TPU v7x, 128 devices: a whole 4x4x4 slice. The times are simulated.
128 devices in a mesh: tm: 8 (over y_lo, x), chan: 16 (over z, y_hi, core).
Axes of the slice: x: 4, y: 4 (y_hi: 2, y_lo: 2; y = y_hi * 2 + y_lo), z: 4, core: 2. Of those that a mesh axis runs over, the one named last changes fastest.
Arguments:
- samples: bfloat16 [1024, 262144], P('tm', 'chan'), may hold values from -6 to 6
- valid: int32 [1024, 32], P('tm', 'chan'), may hold values from 0 to 1, as said below
Outputs:
- average: float32 [1024, 4224], P(('tm', 'chan'))
Inputs may be any that keep to these rules, and one draw needn't show every extreme that they name: `valid`: split the channels into aligned groups of 128; in every segment each group has at most 96 entries equal to 1, and exactly 96 for some group and segment; at least one channel has no 1 in any segment.
All inputs are finite; a program needn't handle non-finite values.
Results may differ from a plain program's by a relative error of at most 0.0026.
Values may be sent and summed in bfloat16 or wider, within the bound.
A program may use at most 128 MiB of HBM per device.

v0:
```python
import jax
import jax.numpy as jnp
from jax import lax
from jax.sharding import PartitionSpec as P

RADIX = 128
KBANDS = 33
full_turn = 6.283185307179586


def make_tables():
    seg_len = RADIX * RADIX
    counter = jnp.arange(RADIX, dtype=jnp.int32)
    inner_prod = counter[:, None] * counter[None, :] % RADIX
    angle_one = full_turn * inner_prod.astype(jnp.float32) / RADIX
    cos_one = jnp.cos(angle_one).astype(jnp.bfloat16)
    sin_one = jnp.sin(angle_one).astype(jnp.bfloat16)
    outer_prod = counter[:, None] * counter[None, :] % seg_len
    angle_mid = full_turn * outer_prod.astype(jnp.float32) / seg_len
    twid_real = jnp.cos(angle_mid)
    twid_imag = -jnp.sin(angle_mid)
    band_index = jnp.arange(KBANDS, dtype=jnp.int32)
    angle_two = (
        full_turn * (counter[:, None] * band_index[None, :] % RADIX).astype(jnp.float32) / RADIX
    )
    cos_two = jnp.cos(angle_two).astype(jnp.bfloat16)
    sine_double_angle = jnp.sin(angle_two).astype(jnp.bfloat16)
    places = jnp.arange(seg_len, dtype=jnp.int32).astype(jnp.float32)
    window = 0.5 - 0.5 * jnp.cos(full_turn * places / seg_len)
    weight_sum = jnp.sum(window * window)
    onesided = (
        jnp.where(jnp.arange(KBANDS * RADIX, dtype=jnp.int32) == 0, 1.0, 2.0).astype(jnp.float32)
        / weight_sum
    )
    return (cos_one, sin_one, twid_real, twid_imag, cos_two, sine_double_angle, window, onesided)


def contract(left, right, form):
    return jnp.einsum(form, left, right, preferred_element_type=jnp.float32)


def spectrum(segment, tables):
    cos_one, sin_one, twid_real, twid_imag, cos_two, sine_double_angle, window, onesided = tables
    height = segment.shape[0]
    values = segment.astype(jnp.float32)
    centred = values - jnp.mean(values, axis=1, keepdims=True)
    shaped = (centred * window[None, :]).astype(jnp.bfloat16).reshape(height, RADIX, RADIX)
    first_real = contract(shaped, cos_one, "cnm,nk->ckm")
    first_imag = -contract(shaped, sin_one, "cnm,nk->ckm")
    mid_real = (first_real * twid_real - first_imag * twid_imag).astype(jnp.bfloat16)
    mid_imag = (first_real * twid_imag + first_imag * twid_real).astype(jnp.bfloat16)
    last_real = contract(mid_real, cos_two, "ckn,nm->cmk") + contract(
        mid_imag, sine_double_angle, "ckn,nm->cmk"
    )
    closing_quadrature_part = contract(mid_imag, cos_two, "ckn,nm->cmk") - contract(
        mid_real, sine_double_angle, "ckn,nm->cmk"
    )
    return (last_real * last_real + closing_quadrature_part * closing_quadrature_part).reshape(
        height, -1
    ) * onesided[None, :]


def block_power(leading, trailing, tables):
    height = leading.shape[0]
    block_rows = 128
    segments = jnp.concatenate([leading, trailing], axis=1)

    def one_block(piece):
        return spectrum(piece, tables)

    final_output = lax.map(one_block, segments.reshape(height // block_rows, block_rows, -1))
    return final_output.reshape(height, -1)


def per_device(samples, valid):
    tables = make_tables()
    half_len = RADIX * RADIX // 2
    moved_samples, moved_valid = (
        lax.all_to_all(samples, "chan", split_axis=0, concat_axis=1, tiled=True),
        lax.all_to_all(valid.astype(jnp.bfloat16), "chan", split_axis=0, concat_axis=1, tiled=True),
    )
    owned_rows = moved_samples.shape[0]
    record = jnp.concatenate(
        [moved_samples, jnp.zeros((owned_rows, half_len), jnp.bfloat16)], axis=1
    )
    blocks = record.reshape(owned_rows, -1, half_len)
    leading = blocks[:, :-1].reshape(-1, half_len)
    trailing = blocks[:, 1:].reshape(-1, half_len)
    powers = block_power(leading, trailing, tables).reshape(owned_rows, blocks.shape[1] - 1, -1)
    weights = moved_valid.astype(jnp.float32)
    totals = jnp.sum(weights[:, :, None] * powers, axis=1)
    tallied_count = jnp.sum(weights, axis=1)
    return totals / jnp.maximum(tallied_count, 1.0)[:, None]


def solution(mesh):
    return jax.shard_map(
        per_device,
        mesh=mesh,
        in_specs=(P("tm", "chan"), P("tm", "chan")),
        out_specs=P(("tm", "chan"), None),
        check_vma=False,
    )
```

profile of v0, /device:TPU:1, one launch (start us, length us, event | category | flops | bytes accessed | tf_op | source)
XLA Modules:
  0.0 189.5 jit_solution(12834739281329465822)
XLA Ops:
  0.8 16.3 %all_to_all.32 = bf16[16,8,2]{1,2,0:T(2,128)(2,1)S(1)} all-to-all(bf16[16,8,2]{1,2,0:T(2,128)(2,1)S(1)} %copy.36), channel_id=1, replica_groups=mesh['tm'=8,'chan'=16] {'chan'}, dimensions={0} | all-to-all | bytes 1024 | tf_op jit(solution)/shard_map/all_to_all | solution.py:80
  17.1 4.9 %all-to-all-start.1 = ((bf16[16,8,16384]{2,1,0:T(8,128)(2,1)}), bf16[16,8,16384]{2,1,0:T(8,128)(2,1)}, u32[]{:S(2)}, u32[]{:S(2)}) async-start(bf16[16,8,16384]{2,1,0:T(8,128)(2,1)} %bitcast.100), calls=%async_computation.1 | async-start | bytes 8388608 | tf_op jit(solution)/shard_map/all_to_all | solution.py:79
  24.0 49.0 %all-to-all-done.1 = bf16[16,8,16384]{2,1,0:T(8,128)(2,1)} async-done(((bf16[16,8,16384]{2,1,0:T(8,128)(2,1)}), bf16[16,8,16384]{2,1,0:T(8,128)(2,1)}, u32[]{:S(2)}, u32[]{:S(2)}) %all-to-all-start.1) | async-done | bytes 4194336 | tf_op jit(solution)/shard_map/all_to_all | solution.py:79
  73.0 3.0 %concatenate.11 = bf16[8,270336]{1,0:T(8,128)(2,1)S(1)} pad(bf16[8,262144]{1,0:T(8,128)(2,1)} %bitcast.4, bf16[]{:T(256)} %constant.69.clone.1), padding=0_0x0_8192 | pad | bytes 8519682 | tf_op jit(solution)/shard_map/concatenate | solution.py:83
  77.0 4.3 %copy.38 = bf16[8,32,8192]{2,1,0:T(8,128)(2,1)} copy(bf16[8,32,8192]{2,0,1:T(8,128)(2,1)S(1)} %get-tuple-element.140) | data formatting | bytes 8388608 | tf_op jit(solution)/shard_map/slice | solution.py:87
  81.2 4.3 %copy.39 = bf16[8,32,8192]{2,1,0:T(8,128)(2,1)} copy(bf16[8,32,8192]{2,0,1:T(8,128)(2,1)S(1)} %get-tuple-element.141) | data formatting | bytes 8388608 | tf_op jit(solution)/shard_map/slice | solution.py:88
  85.5 7.6 %pad_maximum_fusion = bf16[2,128,16384]{2,1,0:T(8,128)(2,1)} fusion(bf16[2,128,8192]{2,1,0:T(8,128)(2,1)} %bitcast.98, bf16[2,128,8192]{2,1,0:T(8,128)(2,1)} %bitcast.97), kind=kLoop, calls=%fused_computation.92 | loop fusion | flops 16777216 | bytes 16777216 | tf_op jit(solution)/shard_map/concatenate | solution.py:66
  93.1 92.8 %while.12 = (s32[]{:T(128)}, f32[2,128,4224]{2,1,0:T(8,128)}, bf16[2,128,16384]{2,1,0:T(8,128)(2,1)}, f32[]{:T(128)}, s32[]{:T(128)}) while((s32[]{:T(128)}, f32[2,128,4224]{2,1,0:T(8,128)}, bf16[2,128,16384]{2,1,0:T(8,128)(2,1)}, f32[]{:T(128)}, s32[]{:T(128)}) %tuple.31), condition=%wide.region_3.4_spmd.clone.clone, body=%wide.region_1.3_spmd.clone.clone.sunk | while | flops 1669451648 | bytes 142118992 | solution.py:71
  93.1 3.0 %convert_bitcast_fusion.2 = f32[16,8,128,128]{3,1,2,0:T(8,128)S(1)} fusion(bf16[2,128,16384]{2,1,0:T(8,128)(2,1)} %get-tuple-element.187, s32[]{:T(128)} %get-tuple-element.180), kind=kLoop, calls=%fused_computation.9.clone.1 | loop fusion | flops 2097152 | bytes 12582916 | tf_op jit(solution)/shard_map/while
  96.1 4.7 %copy.56 = f32[16,8,128,128]{3,2,1,0:T(8,128)} copy(f32[16,8,128,128]{3,1,2,0:T(8,128)S(1)} %convert_bitcast_fusion.2) | data formatting | bytes 16777216 | tf_op jit(solution)/shard_map/while
  100.8 9.0 %copy.57 = f32[128,128,128]{1,2,0:T(8,128)} copy(f32[128,128,128]{2,1,0:T(8,128)} %bitcast.95) | data formatting | bytes 16777216 | tf_op jit(solution)/shard_map/while/body/eval_jaxpr/convert_element_type | solution.py:45
  109.8 2.8 %convert_reduce_fusion.3 = f32[128]{0:T(128)S(1)} fusion(bf16[2,128,16384]{2,1,0:T(8,128)(2,1)} %get-tuple-element.187, s32[]{:T(128)} %get-tuple-element.180), kind=kLoop, calls=%fused_computation.8.clone.1 | loop fusion | flops 4194176 | bytes 4194820 | tf_op jit(solution)/shard_map/while/body/eval_jaxpr/reduce_sum | solution.py:46
  112.9 4.9 %fusion.108 = f32[128,128,128]{2,1,0:T(8,128)S(1)} fusion(f32[128,128,128]{1,2,0:T(8,128)} %copy.57, f32[128,128]{0,1:T(8,128)S(1)} %copy.58, f32[128]{0:T(128)S(1)} %broadcast_multiply_fusion.2), kind=kOutput, calls=%fused_computation.46.clone.1 | convolution fusion | flops 543408128 | bytes 16843264 | tf_op jit(solution)/shard_map/while/body/eval_jaxpr/cnm,nk->ckm/dot_general | solution.py:39
  118.1 7.1 %fusion.109 = (bf16[128,128,128]{1,2,0:T(8,128)(2,1)S(1)}, bf16[128,128,128]{1,2,0:T(8,128)(2,1)S(1)}) fusion(f32[128,128,128]{2,1,0:T(8,128)S(1)} %fusion.108, f32[128,128]{0,1:T(8,128)S(1)} %get-tuple-element.171, f32[128,128]{0,1:T(8,128)S(1)} %get-tuple-element.172, f32[128,128,128]{1,2,0:T(8,128)} %copy.57, f32[128,128]{0,1:T(8,128)S(1)} %copy.58, ...), kind=kOutput, calls=%fused_computation.13.clone.1 | convolution fusion | flops 562282496 | bytes 25362944 | tf_op jit(solution)/shard_map/while/body/eval_jaxpr/cnm,nk->ckm/dot_general | solution.py:39
  131.3 3.0 %bitcast_multiply_fusion.6 = f32[1,128,4224]{1,2,0:T(8,128)S(1)} fusion(f32[128,33,128]{0,2,1:T(8,128)} %copy.59, f32[4224]{0:T(1024)S(1)} %select_divide_fusion.2), kind=kLoop, calls=%fused_computation.20.clone.1 | loop fusion | flops 540672 | bytes 4342272 | tf_op jit(solution)/shard_map/while/body/eval_jaxpr/mul | solution.py:58
  136.4 3.1 %constant_dynamic-update-slice_fusion.2 = f32[2,128,4224]{2,1,0:T(8,128)} fusion(f32[2,128,4224]{2,1,0:T(8,128)} %get-tuple-element.181, f32[1,128,4224]{2,1,0:T(8,128)} %copy.60, s32[]{:T(128)} %get-tuple-element.180), kind=kLoop, calls=%fused_computation.72.clone.1 | loop fusion | bytes 4325888 | tf_op jit(solution)/shard_map/while/body/jit(dynamic_update_index_in_dim)/dynamic_update_slice | solution.py:71
  139.5 3.0 %convert_bitcast_fusion.2 = f32[16,8,128,128]{3,1,2,0:T(8,128)S(1)} fusion(bf16[2,128,16384]{2,1,0:T(8,128)(2,1)} %get-tuple-element.187, s32[]{:T(128)} %get-tuple-element.180), kind=kLoop, calls=%fused_computation.9.clone.1 | loop fusion | flops 2097152 | bytes 12582916 | tf_op jit(solution)/shard_map/while
  142.5 4.7 %copy.56 = f32[16,8,128,128]{3,2,1,0:T(8,128)} copy(f32[16,8,128,128]{3,1,2,0:T(8,128)S(1)} %convert_bitcast_fusion.2) | data formatting | bytes 16777216 | tf_op jit(solution)/shard_map/while
  147.2 9.0 %copy.57 = f32[128,128,128]{1,2,0:T(8,128)} copy(f32[128,128,128]{2,1,0:T(8,128)} %bitcast.95) | data formatting | bytes 16777216 | tf_op jit(solution)/shard_map/while/body/eval_jaxpr/convert_element_type | solution.py:45
  159.4 4.9 %fusion.108 = f32[128,128,128]{2,1,0:T(8,128)S(1)} fusion(f32[128,128,128]{1,2,0:T(8,128)} %copy.57, f32[128,128]{0,1:T(8,128)S(1)} %copy.58, f32[128]{0:T(128)S(1)} %broadcast_multiply_fusion.2), kind=kOutput, calls=%fused_computation.46.clone.1 | convolution fusion | flops 543408128 | bytes 16843264 | tf_op jit(solution)/shard_map/while/body/eval_jaxpr/cnm,nk->ckm/dot_general | solution.py:39
  164.6 7.1 %fusion.109 = (bf16[128,128,128]{1,2,0:T(8,128)(2,1)S(1)}, bf16[128,128,128]{1,2,0:T(8,128)(2,1)S(1)}) fusion(f32[128,128,128]{2,1,0:T(8,128)S(1)} %fusion.108, f32[128,128]{0,1:T(8,128)S(1)} %get-tuple-element.171, f32[128,128]{0,1:T(8,128)S(1)} %get-tuple-element.172, f32[128,128,128]{1,2,0:T(8,128)} %copy.57, f32[128,128]{0,1:T(8,128)S(1)} %copy.58, ...), kind=kOutput, calls=%fused_computation.13.clone.1 | convolution fusion | flops 562282496 | bytes 25362944 | tf_op jit(solution)/shard_map/while/body/eval_jaxpr/cnm,nk->ckm/dot_general | solution.py:39
  177.7 3.0 %bitcast_multiply_fusion.6 = f32[1,128,4224]{1,2,0:T(8,128)S(1)} fusion(f32[128,33,128]{0,2,1:T(8,128)} %copy.59, f32[4224]{0:T(1024)S(1)} %select_divide_fusion.2), kind=kLoop, calls=%fused_computation.20.clone.1 | loop fusion | flops 540672 | bytes 4342272 | tf_op jit(solution)/shard_map/while/body/eval_jaxpr/mul | solution.py:58
  182.8 3.1 %constant_dynamic-update-slice_fusion.2 = f32[2,128,4224]{2,1,0:T(8,128)} fusion(f32[2,128,4224]{2,1,0:T(8,128)} %get-tuple-element.181, f32[1,128,4224]{2,1,0:T(8,128)} %copy.60, s32[]{:T(128)} %get-tuple-element.180), kind=kLoop, calls=%fused_computation.72.clone.1 | loop fusion | bytes 4325888 | tf_op jit(solution)/shard_map/while/body/jit(dynamic_update_index_in_dim)/dynamic_update_slice | solution.py:71
  185.9 2.8 %multiply_reduce_fusion = f32[8,4224]{1,0:T(8,128)S(1)} fusion(f32[8,32,4224]{2,1,0:T(8,128)} %bitcast.99, f32[8,32]{1,0:T(8,128)S(1)} %copy-done), kind=kLoop, calls=%fused_computation.93 | loop fusion | flops 2128896 | bytes 4461568 | tf_op jit(solution)/shard_map/reduce_sum | solution.py:91
  (38 shorter events, 24.6 us)
Async XLA Ops:
  17.1 55.9 %all-to-all-start.1 = ((bf16[16,8,16384]{2,1,0:T(8,128)(2,1)}), bf16[16,8,16384]{2,1,0:T(8,128)(2,1)}, u32[]{:S(2)}, u32[]{:S(2)}) async-start(bf16[16,8,16384]{2,1,0:T(8,128)(2,1)} %bitcast.100), calls=%async_computation.1 | async-start | bytes 8388608 | tf_op jit(solution)/shard_map/all_to_all | solution.py:79
  93.1 92.9 %copy-start = (f32[8,32]{1,0:T(8,128)S(1)}, f32[8,32]{1,0:T(8,128)}, u32[]{:S(2)}) copy-start(f32[8,32]{1,0:T(8,128)} %copy.37) | copy-start | bytes 3076
  185.9 2.8 %copy-start.1 = (f32[8]{0:T(128)S(1)}, f32[8]{0:T(128)}, u32[]{:S(2)}) copy-start(f32[8]{0:T(128)} %broadcast_maximum_fusion) | copy-start | bytes 100
where the time goes:
time: 191 us; the launch traced here: 189 us
  local copies, waits for them, and re-layouts  55.3 us (29%)
  waiting for transfers between devices  49 us (26%)
  other arithmetic  33.2 us (17%)
  matrix products  30.6 us (16%)
  blocking collectives  16.3 us (9%)
  starting transfers between devices  4.93 us (3%)
    all_to_all x1, waiting for transfers between devices, per_device(): lax.all_to_all(samples, 'chan', split_axis=0, concat_axis=1, tiled=True)  49 us
    dot_general x12, matrix products, contract(): return jnp.einsum(form, left, right, preferred_element_type=jnp.float32)  30.6 us
    convert_element_type x2, local copies, waits for them, and re-layouts, spectrum(): values = segment.astype(jnp.float32)  18 us
    all_to_all x1, blocking collectives, per_device(): lax.all_to_all(valid.astype(jnp.bfloat16), 'chan', split_axis=0, concat_a...  16.3 us
    dynamic_update_slice x4, local copies, waits for them, and re-layouts, block_power(): lax.map(one_block, segments.reshape(height // block_rows, block_rows, -1))  10.4 us
    while x2, local copies, waits for them, and re-layouts  9.36 us
    concatenate x1, other arithmetic, block_power(): segments = jnp.concatenate([leading, trailing], axis=1)  7.56 us
    mul x2, other arithmetic, spectrum(): (last_real * last_real + closing_quadrature_part * closing_quadrature_par...  6.09 us
  transfers between devices with their start and end apart: 1, of which 1 were waited for; matrix products, arithmetic and copies ran while one was open for 1% of the time, Pallas kernels for 0%

commit v1 on v0

--- a/solution.py
+++ b/solution.py
@@ -2,6 +2,7 @@
 import jax.numpy as jnp
 from jax import lax
 from jax.sharding import PartitionSpec as P
+from jax.lax import all_to_all, axis_size
 
 RADIX = 128
 KBANDS = 33
@@ -77,7 +78,15 @@
     half_len = RADIX * RADIX // 2
     moved_samples, moved_valid = (
         lax.all_to_all(samples, "chan", split_axis=0, concat_axis=1, tiled=True),
-        lax.all_to_all(valid.astype(jnp.bfloat16), "chan", split_axis=0, concat_axis=1, tiled=True),
+        jnp.concatenate(
+            all_to_all(
+                jnp.stack(jnp.split(valid.astype(jnp.bfloat16), axis_size("chan"), 0)),
+                axis_name="chan",
+                split_axis=0,
+                concat_axis=0,
+            ),
+            1,
+        ),
     )
     owned_rows = moved_samples.shape[0]
     record = jnp.concatenate(

time: 191 us -> 197 us (1.031)
  matrix products: 30.6 us -> 35.8 us
    dot_general x12, matrix products: 30.6 us -> 35.8 us  [contract(): return jnp.einsum(form, left, right, preferred_element_type=jnp.float32)]
    while x2 -> x10, local copies, waits for them, and re-layouts: 9.36 us -> 9.39 us
    while x2 -> x4, other arithmetic: 6.05 us -> 6.06 us
where the time goes in v1:
time: 197 us; the launch traced here: 196 us
  local copies, waits for them, and re-layouts  56.4 us (29%)
  waiting for transfers between devices  49 us (25%)
  matrix products  35.8 us (18%)
  other arithmetic  33.1 us (17%)
  blocking collectives  16.2 us (8%)
  starting transfers between devices  4.93 us (3%)
    all_to_all x1, waiting for transfers between devices, per_device(): lax.all_to_all(samples, 'chan', split_axis=0, concat_axis=1, tiled=True)  49 us
    dot_general x12, matrix products, contract(): return jnp.einsum(form, left, right, preferred_element_type=jnp.float32)  35.8 us
    convert_element_type x2, local copies, waits for them, and re-layouts, spectrum(): values = segment.astype(jnp.float32)  18 us
    all_to_all x1, blocking collectives, per_device(): all_to_all(jnp.stack(jnp.split(valid.astype(jnp.bfloat16), axis_size('cha...  16.2 us
    dynamic_update_slice x4, local copies, waits for them, and re-layouts, block_power(): lax.map(one_block, segments.reshape(height // block_rows, block_rows, -1))  10.3 us
    while x10, local copies, waits for them, and re-layouts  9.39 us
    concatenate x1, other arithmetic, block_power(): segments = jnp.concatenate([leading, trailing], axis=1)  7.56 us
    mul x2, other arithmetic, spectrum(): (last_real * last_real + closing_quadrature_part * closing_quadrature_par...  6.09 us
  transfers between devices with their start and end apart: 1, of which 1 were waited for; matrix products, arithmetic and copies ran while one was open for 1% of the time, Pallas kernels for 0%

profile of v1, /device:TPU:1, one launch (start us, length us, event | category | flops | bytes accessed | tf_op | source)
XLA Modules:
  0.0 195.7 jit_solution(7876116745931648055)
XLA Ops:
  1.9 16.2 %all_to_all.24 = bf16[16,8,2]{1,2,0:T(2,128)(2,1)S(1)} all-to-all(bf16[16,8,2]{1,2,0:T(2,128)(2,1)S(1)} %constant_dynamic-update-slice_fusion.1), channel_id=1, replica_groups=mesh['tm'=8,'chan'=16] {'chan'}, dimensions={0} | all-to-all | bytes 1024 | tf_op jit(solution)/shard_map/all_to_all | solution.py:82
  18.1 4.9 %all-to-all-start.1 = ((bf16[16,8,16384]{2,1,0:T(8,128)(2,1)}), bf16[16,8,16384]{2,1,0:T(8,128)(2,1)}, u32[]{:S(2)}, u32[]{:S(2)}) async-start(bf16[16,8,16384]{2,1,0:T(8,128)(2,1)} %bitcast.132), calls=%async_computation.1 | async-start | bytes 8388608 | tf_op jit(solution)/shard_map/all_to_all | solution.py:80
  25.1 49.0 %all-to-all-done.1 = bf16[16,8,16384]{2,1,0:T(8,128)(2,1)} async-done(((bf16[16,8,16384]{2,1,0:T(8,128)(2,1)}), bf16[16,8,16384]{2,1,0:T(8,128)(2,1)}, u32[]{:S(2)}, u32[]{:S(2)}) %all-to-all-start.1) | async-done | bytes 4194336 | tf_op jit(solution)/shard_map/all_to_all | solution.py:80
  74.1 3.0 %concatenate.11 = bf16[8,270336]{1,0:T(8,128)(2,1)S(1)} pad(bf16[8,262144]{1,0:T(8,128)(2,1)} %bitcast.20, bf16[]{:T(256)} %constant.69.clone.1), padding=0_0x0_8192 | pad | bytes 8519682 | tf_op jit(solution)/shard_map/concatenate | solution.py:92
  78.0 4.3 %copy.26 = bf16[8,32,8192]{2,1,0:T(8,128)(2,1)} copy(bf16[8,32,8192]{2,0,1:T(8,128)(2,1)S(1)} %get-tuple-element.141) | data formatting | bytes 8388608 | tf_op jit(solution)/shard_map/slice | solution.py:97
  82.3 4.2 %copy.25 = bf16[8,32,8192]{2,1,0:T(8,128)(2,1)} copy(bf16[8,32,8192]{2,0,1:T(8,128)(2,1)S(1)} %get-tuple-element.140) | data formatting | bytes 8388608 | tf_op jit(solution)/shard_map/slice | solution.py:96
  86.6 7.6 %pad_maximum_fusion = bf16[2,128,16384]{2,1,0:T(8,128)(2,1)} fusion(bf16[2,128,8192]{2,1,0:T(8,128)(2,1)} %bitcast.129, bf16[2,128,8192]{2,1,0:T(8,128)(2,1)} %bitcast.130), kind=kLoop, calls=%fused_computation.92 | loop fusion | flops 16777216 | bytes 16777216 | tf_op jit(solution)/shard_map/concatenate | solution.py:67
  94.1 98.0 %while.12 = (s32[]{:T(128)}, f32[2,128,4224]{2,1,0:T(8,128)}, bf16[2,128,16384]{2,1,0:T(8,128)(2,1)}, f32[]{:T(128)}, s32[]{:T(128)}) while((s32[]{:T(128)}, f32[2,128,4224]{2,1,0:T(8,128)}, bf16[2,128,16384]{2,1,0:T(8,128)(2,1)}, f32[]{:T(128)}, s32[]{:T(128)}) %tuple.31), condition=%wide.region_3.4_spmd.clone.clone, body=%wide.region_1.3_spmd.clone.clone.sunk | while | flops 1669451648 | bytes 167284368 | solution.py:72
  94.1 3.0 %convert_bitcast_fusion.2 = f32[16,8,128,128]{3,1,2,0:T(8,128)S(1)} fusion(bf16[2,128,16384]{2,1,0:T(8,128)(2,1)} %get-tuple-element.187, s32[]{:T(128)S(6)} %copy.51), kind=kLoop, calls=%fused_computation.9.clone.1 | loop fusion | flops 2097152 | bytes 12582916 | tf_op jit(solution)/shard_map/while
  97.2 4.7 %copy.43 = f32[16,8,128,128]{3,2,1,0:T(8,128)} copy(f32[16,8,128,128]{3,1,2,0:T(8,128)S(1)} %convert_bitcast_fusion.2) | data formatting | bytes 16777216 | tf_op jit(solution)/shard_map/while
  101.8 9.0 %copy.44 = f32[128,128,128]{1,2,0:T(8,128)} copy(f32[128,128,128]{2,1,0:T(8,128)} %bitcast.127) | data formatting | bytes 16777216 | tf_op jit(solution)/shard_map/while/body/eval_jaxpr/convert_element_type | solution.py:46
  111.2 2.8 %convert_reduce_fusion.3 = f32[128]{0:T(128)S(1)} fusion(bf16[2,128,16384]{2,1,0:T(8,128)(2,1)} %get-tuple-element.187, s32[]{:T(128)S(6)} %copy.51), kind=kLoop, calls=%fused_computation.8.clone.1 | loop fusion | flops 4194176 | bytes 4194820 | tf_op jit(solution)/shard_map/while/body/eval_jaxpr/reduce_sum | solution.py:47
  114.0 8.3 %fusion.108 = f32[128,128,128]{2,1,0:T(8,128)} fusion(f32[128,128,128]{1,2,0:T(8,128)} %copy.44, f32[128,128]{0,1:T(8,128)S(1)} %copy.45, f32[128]{0:T(128)S(1)} %broadcast_multiply_fusion.2), kind=kOutput, calls=%fused_computation.46.clone.1 | convolution fusion | flops 543408128 | bytes 16843264 | tf_op jit(solution)/shard_map/while/body/eval_jaxpr/cnm,nk->ckm/dot_general | solution.py:40
  122.6 6.4 %fusion.109 = (bf16[128,128,128]{1,2,0:T(8,128)(2,1)S(1)}, bf16[128,128,128]{1,2,0:T(8,128)(2,1)S(1)}) fusion(f32[128,128,128]{2,1,0:T(8,128)} %fusion.108, f32[128,128]{0,1:T(8,128)S(1)} %get-tuple-element.171, f32[128,128]{0,1:T(8,128)S(1)} %get-tuple-element.172, f32[128,128,128]{1,2,0:T(8,128)S(1)} %bitcast.126, f32[128,128]{0,1:T(8,128)S(1)} %copy.45, ...), kind=kOutput, calls=%fused_computation.13.clone.1 | convolution fusion | flops 562282496 | bytes 25362944 | tf_op jit(solution)/shard_map/while/body/eval_jaxpr/cnm,nk->ckm/dot_general | solution.py:40
  134.9 3.0 %bitcast_multiply_fusion.6 = f32[1,128,4224]{1,2,0:T(8,128)S(1)} fusion(f32[128,33,128]{0,2,1:T(8,128)} %copy.46, f32[4224]{0:T(1024)S(1)} %select_divide_fusion.2), kind=kLoop, calls=%fused_computation.20.clone.1 | loop fusion | flops 540672 | bytes 4342272 | tf_op jit(solution)/shard_map/while/body/eval_jaxpr/mul | solution.py:59
  140.0 3.1 %constant_dynamic-update-slice_fusion.18 = f32[2,128,4224]{2,1,0:T(8,128)} fusion(f32[2,128,4224]{2,1,0:T(8,128)} %get-tuple-element.181, f32[1,128,4224]{2,1,0:T(8,128)} %copy.47, s32[]{:T(128)S(6)} %copy.51), kind=kLoop, calls=%fused_computation.72.clone.1 | loop fusion | bytes 4325380 | tf_op jit(solution)/shard_map/while/body/jit(dynamic_update_index_in_dim)/dynamic_update_slice | solution.py:72
  143.2 3.0 %convert_bitcast_fusion.2 = f32[16,8,128,128]{3,1,2,0:T(8,128)S(1)} fusion(bf16[2,128,16384]{2,1,0:T(8,128)(2,1)} %get-tuple-element.187, s32[]{:T(128)S(6)} %copy.51), kind=kLoop, calls=%fused_computation.9.clone.1 | loop fusion | flops 2097152 | bytes 12582916 | tf_op jit(solution)/shard_map/while
  146.2 4.7 %copy.43 = f32[16,8,128,128]{3,2,1,0:T(8,128)} copy(f32[16,8,128,128]{3,1,2,0:T(8,128)S(1)} %convert_bitcast_fusion.2) | data formatting | bytes 16777216 | tf_op jit(solution)/shard_map/while
  150.9 9.0 %copy.44 = f32[128,128,128]{1,2,0:T(8,128)} copy(f32[128,128,128]{2,1,0:T(8,128)} %bitcast.127) | data formatting | bytes 16777216 | tf_op jit(solution)/shard_map/while/body/eval_jaxpr/convert_element_type | solution.py:46
  163.1 8.3 %fusion.108 = f32[128,128,128]{2,1,0:T(8,128)} fusion(f32[128,128,128]{1,2,0:T(8,128)} %copy.44, f32[128,128]{0,1:T(8,128)S(1)} %copy.45, f32[128]{0:T(128)S(1)} %broadcast_multiply_fusion.2), kind=kOutput, calls=%fused_computation.46.clone.1 | convolution fusion | flops 543408128 | bytes 16843264 | tf_op jit(solution)/shard_map/while/body/eval_jaxpr/cnm,nk->ckm/dot_general | solution.py:40
  171.7 6.4 %fusion.109 = (bf16[128,128,128]{1,2,0:T(8,128)(2,1)S(1)}, bf16[128,128,128]{1,2,0:T(8,128)(2,1)S(1)}) fusion(f32[128,128,128]{2,1,0:T(8,128)} %fusion.108, f32[128,128]{0,1:T(8,128)S(1)} %get-tuple-element.171, f32[128,128]{0,1:T(8,128)S(1)} %get-tuple-element.172, f32[128,128,128]{1,2,0:T(8,128)S(1)} %bitcast.126, f32[128,128]{0,1:T(8,128)S(1)} %copy.45, ...), kind=kOutput, calls=%fused_computation.13.clone.1 | convolution fusion | flops 562282496 | bytes 25362944 | tf_op jit(solution)/shard_map/while/body/eval_jaxpr/cnm,nk->ckm/dot_general | solution.py:40
  183.9 3.0 %bitcast_multiply_fusion.6 = f32[1,128,4224]{1,2,0:T(8,128)S(1)} fusion(f32[128,33,128]{0,2,1:T(8,128)} %copy.46, f32[4224]{0:T(1024)S(1)} %select_divide_fusion.2), kind=kLoop, calls=%fused_computation.20.clone.1 | loop fusion | flops 540672 | bytes 4342272 | tf_op jit(solution)/shard_map/while/body/eval_jaxpr/mul | solution.py:59
  189.0 3.1 %constant_dynamic-update-slice_fusion.18 = f32[2,128,4224]{2,1,0:T(8,128)} fusion(f32[2,128,4224]{2,1,0:T(8,128)} %get-tuple-element.181, f32[1,128,4224]{2,1,0:T(8,128)} %copy.47, s32[]{:T(128)S(6)} %copy.51), kind=kLoop, calls=%fused_computation.72.clone.1 | loop fusion | bytes 4325380 | tf_op jit(solution)/shard_map/while/body/jit(dynamic_update_index_in_dim)/dynamic_update_slice | solution.py:72
  192.1 2.8 %multiply_reduce_fusion = f32[8,4224]{1,0:T(8,128)S(1)} fusion(f32[8,32,4224]{2,1,0:T(8,128)} %bitcast.131, f32[8,32]{1,0:T(8,128)S(1)} %copy-done), kind=kLoop, calls=%fused_computation.93 | loop fusion | flops 2128896 | bytes 4461568 | tf_op jit(solution)/shard_map/reduce_sum | solution.py:100
  (62 shorter events, 25.5 us)
Async XLA Ops:
  18.1 55.9 %all-to-all-start.1 = ((bf16[16,8,16384]{2,1,0:T(8,128)(2,1)}), bf16[16,8,16384]{2,1,0:T(8,128)(2,1)}, u32[]{:S(2)}, u32[]{:S(2)}) async-start(bf16[16,8,16384]{2,1,0:T(8,128)(2,1)} %bitcast.132), calls=%async_computation.1 | async-start | bytes 8388608 | tf_op jit(solution)/shard_map/all_to_all | solution.py:80
  94.1 98.0 %copy-start = (f32[8,32]{1,0:T(8,128)S(1)}, f32[8,32]{1,0:T(8,128)}, u32[]{:S(2)}) copy-start(f32[8,32]{1,0:T(8,128)} %copy.24) | copy-start | bytes 3076
  114.0 8.6 %slice-start = ((s8[8388608]{0:T(1024)(128)(4,1)}), s8[4194304]{0:T(1024)(128)(4,1)S(1)}, s32[]{:S(2)}) async-start(s8[8388608]{0:T(1024)(128)(4,1)} %bitcast.125), calls=%async_computation.2 | async-start | bytes 8388608 | tf_op jit(solution)/shard_map/while
  114.0 8.6 %slice-start.1 = ((s8[8388608]{0:T(1024)(128)(4,1)}), s8[4194304]{0:T(1024)(128)(4,1)S(1)}, s32[]{:S(2)}) async-start(s8[8388608]{0:T(1024)(128)(4,1)} %bitcast.125), calls=%async_computation.3 | async-start | bytes 8388608 | tf_op jit(solution)/shard_map/while
  163.0 8.6 %slice-start = ((s8[8388608]{0:T(1024)(128)(4,1)}), s8[4194304]{0:T(1024)(128)(4,1)S(1)}, s32[]{:S(2)}) async-start(s8[8388608]{0:T(1024)(128)(4,1)} %bitcast.125), calls=%async_computation.2 | async-start | bytes 8388608 | tf_op jit(solution)/shard_map/while
  163.0 8.6 %slice-start.1 = ((s8[8388608]{0:T(1024)(128)(4,1)}), s8[4194304]{0:T(1024)(128)(4,1)S(1)}, s32[]{:S(2)}) async-start(s8[8388608]{0:T(1024)(128)(4,1)} %bitcast.125), calls=%async_computation.3 | async-start | bytes 8388608 | tf_op jit(solution)/shard_map/while
  192.1 2.8 %copy-start.1 = (f32[8]{0:T(128)S(1)}, f32[8]{0:T(128)}, u32[]{:S(2)}) copy-start(f32[8]{0:T(128)} %broadcast_maximum_fusion) | copy-start | bytes 100
